TPU v7x, 512 devices: a whole 4x4x16 slice. The times are simulated.
512 devices in a mesh: row: 32 (over z, core), col: 16 (over x, y).
Axes of the slice: x: 4, y: 4, z: 16, core: 2. Of those that a mesh axis runs over, the one named last changes fastest.
Arguments:
- records: float32 [9, 4096], P(None, 'row'), may hold values from -0.3 to 703, as said below
- pattern: int32 [32, 32], replicated, may hold values from 0 to 1, as said below
- iterate: float32 [4096, 4096], P('row', 'col'), may hold values from -0.5 to 0.5, as said below
Outputs:
- margin: float32 [4096, 4096], P('row', 'col')
- updated: float32 [4096, 4096], P('row', 'col')
Inputs may be any that keep to these rules, and one draw needn't show every extreme that they name: `pattern`: symmetric 0 or 1 entries; the diagonal and the first off-diagonals are 1. `records`: exponents and coefficients are positive. `iterate`: symmetric.
All inputs are finite; a program needn't handle non-finite values.
Results may differ from a plain program's by a relative error of at most 0.0003.
Values sent between devices are 32-bit elements; how exact they have to be, the bound alone decides.
No kernel may reach another device: no remote copies, remote signals or barrier semaphores. Data moves between devices by JAX's collectives and lax.ppermute only.
A program may use at most 64 MiB of HBM per device.

v0:
```python
import jax
import jax.numpy as jnp
from jax import lax
from jax.sharding import PartitionSpec as P

BLOCK = 128
PRIMS = 3


def expand(blocks, size):
    row_blocks, col_blocks = blocks.shape
    grown = jnp.broadcast_to(blocks[:, None, :, None], (row_blocks, size, col_blocks, size))
    return grown.reshape(row_blocks * size, col_blocks * size).astype(jnp.float32)


def pair_margin(left, right):
    distance = (left[0][:, None] - right[0][None, :]) ** 2
    distance = distance + (left[1][:, None] - right[1][None, :]) ** 2
    distance = distance + (left[2][:, None] - right[2][None, :]) ** 2
    accumulated = jnp.zeros(distance.shape, jnp.float32)
    for p in range(PRIMS):
        for q in range(PRIMS):
            exponent_a = left[3 + p][:, None]
            exponent_b = right[3 + q][None, :]
            summed = exponent_a + exponent_b
            prefactor = (2.0 * jnp.sqrt(exponent_a * exponent_b) / summed) ** 1.5
            weight_ab = left[3 + PRIMS + p][:, None] * right[3 + PRIMS + q][None, :]
            accumulated = accumulated + weight_ab * prefactor * jnp.exp(
                -(exponent_a * exponent_b / summed) * distance
            )
    return accumulated


def self_norm(recs):
    accumulated = jnp.zeros(recs.shape[1], jnp.float32)
    for p in range(PRIMS):
        for q in range(PRIMS):
            exponent_a = recs[3 + p]
            exponent_b = recs[3 + q]
            prefactor = (2.0 * jnp.sqrt(exponent_a * exponent_b) / (exponent_a + exponent_b)) ** 1.5
            accumulated = accumulated + recs[3 + PRIMS + p] * recs[3 + PRIMS + q] * prefactor
    return accumulated


def matmul(left, right):
    return jnp.dot(left, right, precision=lax.Precision.HIGHEST, preferred_element_type=jnp.float32)


def accumulate(left, piece):
    return matmul(left, piece)


def body(records, pattern, iterate):
    row_idx = lax.axis_index("row")
    col_idx = lax.axis_index("col")
    row_count, col_count = iterate.shape
    row_blocks = row_count // BLOCK
    col_blocks = col_count // BLOCK
    everyone = lax.all_gather(records, "row", axis=1, tiled=True)
    col_records = lax.dynamic_slice_in_dim(everyone, col_idx * col_count, col_count, 1)
    row_norms = self_norm(records)
    col_norms = self_norm(col_records)
    tile_blocks = lax.dynamic_slice(
        pattern, (row_idx * row_blocks, col_idx * col_blocks), (row_blocks, col_blocks)
    )
    tile_mask = expand(tile_blocks, BLOCK)
    margin = tile_mask * (
        pair_margin(records, col_records) / jnp.sqrt(row_norms[:, None] * col_norms[None, :])
    )
    masked = tile_mask * iterate
    margin_row = lax.all_gather(margin, "col", axis=1, tiled=True)
    iterate_row = lax.all_gather(masked, "col", axis=1, tiled=True)
    iterate_col = lax.all_gather(masked, "row", axis=0, tiled=True)
    product_one = tile_mask * matmul(margin_row, iterate_col)
    product_two = tile_mask * accumulate(
        iterate_row, lax.all_gather(product_one, "row", axis=0, tiled=True)
    )
    second_row = lax.all_gather(product_two, "col", axis=1, tiled=True)
    product_three = matmul(second_row, iterate_col)
    updated = tile_mask * (1.5 * masked - 0.5 * product_three)
    return (margin, updated)


def solution(mesh):
    in_specs = (P(None, "row"), P(), P("row", "col"))
    out_specs = (P("row", "col"), P("row", "col"))
    return jax.shard_map(body, mesh=mesh, in_specs=in_specs, out_specs=out_specs, check_vma=False)
```

profile of v0, /device:TPU:2, one launch (start us, length us, event | category | flops | bytes accessed | tf_op | source)
XLA Modules:
  0.0 397.7 jit_solution(15753159277731944957)
XLA Ops:
  7.2 0.0 all-gather.8.cloned.1.call-start
  7.2 0.9 multiply_add_fusion.1
  8.1 1.0 slice_bitcast_fusion.8
  9.1 37.2 %all_gather.18 = f32[9,4096]{1,0:T(8,128)S(1)} all-gather(f32[9,128]{1,0:T(8,128)} %param.3), channel_id=1, replica_groups=mesh['row'=32,'col'=16] {'row'}, dimensions={1}, use_global_device_ids=true | all-gather | bytes 152064 | tf_op jit(solution)/shard_map/all_gather | solution.py:59
  46.3 0.8 convert_bitcast_fusion
  47.1 0.1 broadcast_bitcast_fusion
  47.1 0.1 constant_dynamic-slice_fusion
  47.3 2.1 fusion.74
  49.4 0.0 all-gather.10.cloned.1.call-start
  49.5 0.7 broadcast_multiply_fusion
  50.2 0.0 all-gather.10.cloned.1.call-update
  50.2 0.0 all-gather.6.cloned.1.call-start
  50.3 0.7 all-gather.6.cloned.1.call-update
  50.9 0.0 all-gather.12.cloned.1.call-start
  51.0 56.6 %all-gather.8.cloned.1.call-done = f32[128,4096]{1,0:T(8,128)} async-done(((f32[128,256]{1,0:T(8,128)}), f32[128,4096]{1,0:T(8,128)}) %all-gather.8.cloned.1.call-update) | async-done | bytes 2097168 | tf_op jit(solution)/shard_map/all_gather | solution.py:71
  107.6 75.9 %all-gather.10.cloned.1.call-done = f32[4096,256]{1,0:T(8,128)} async-done(((f32[128,256]{1,0:T(8,128)}), f32[4096,256]{1,0:T(8,128)}) %all-gather.10.cloned.1.call-update) | async-done | bytes 4194320 | tf_op jit(solution)/shard_map/all_gather | solution.py:73
  183.4 5.6 %convolution_multiply_fusion.2 = f32[128,256]{1,0:T(8,128)} fusion(f32[128,4096]{1,0:T(8,128)} %all-gather.8.cloned.1.call-done, f32[4096,256]{1,0:T(8,128)} %all-gather.10.cloned.1.call-done, f32[256]{0:T(256)S(1)} %broadcast_bitcast_fusion), kind=kOutput, calls=%fused_computation.4 | convolution fusion | flops 1610645504 | bytes 6423552 | tf_op jit(solution)/shard_map/dot_general | solution.py:46
  189.0 0.0 all-gather.12.cloned.1.call-update
  189.1 0.0 all-gather.14.cloned.1.call-start
  189.1 56.8 %all-gather.6.cloned.1.call-done = f32[128,4096]{1,0:T(8,128)} async-done(((f32[128,256]{1,0:T(8,128)}), f32[128,4096]{1,0:T(8,128)}) %all-gather.6.cloned.1.call-update) | async-done | bytes 2097168 | tf_op jit(solution)/shard_map/all_gather | solution.py:72
  245.9 75.1 %all-gather.12.cloned.1.call-done = f32[4096,256]{1,0:T(8,128)} async-done(((f32[128,256]{1,0:T(8,128)}), f32[4096,256]{1,0:T(8,128)}) %all-gather.12.cloned.1.call-update) | async-done | bytes 4194320 | tf_op jit(solution)/shard_map/all_gather | solution.py:76
  321.0 5.6 %convolution_multiply_fusion.1 = f32[128,256]{1,0:T(8,128)} fusion(f32[128,4096]{1,0:T(8,128)} %all-gather.6.cloned.1.call-done, f32[4096,256]{1,0:T(8,128)} %all-gather.12.cloned.1.call-done, f32[256]{0:T(256)S(1)} %broadcast_bitcast_fusion), kind=kOutput, calls=%fused_computation.3 | convolution fusion | flops 1610645504 | bytes 6423552 | tf_op jit(solution)/shard_map/dot_general | solution.py:46
  326.6 59.0 %all-gather.14.cloned.1.call-done = f32[128,4096]{1,0:T(8,128)} async-done(((f32[128,256]{1,0:T(8,128)}), f32[128,4096]{1,0:T(8,128)}) %all-gather.14.cloned.1.call-update) | async-done | bytes 2097168 | tf_op jit(solution)/shard_map/all_gather | solution.py:78
  385.6 5.6 %fusion.1 = f32[128,256]{1,0:T(8,128)} fusion(f32[128,4096]{1,0:T(8,128)} %all-gather.14.cloned.1.call-done, f32[4096,256]{1,0:T(8,128)} %all-gather.10.cloned.1.call-done, f32[256]{0:T(256)S(1)} %broadcast_bitcast_fusion, f32[128,256]{1,0:T(8,128)S(1)} %copy-done), kind=kOutput, calls=%fused_computation.2 | convolution fusion | flops 1610776576 | bytes 6554624 | tf_op jit(solution)/shard_map/dot_general | solution.py:46
  (4 shorter events, 0.0 us)
Async XLA Ops:
  7.2 42.3 %copy-start = (f32[128,256]{1,0:T(8,128)S(1)}, f32[128,256]{1,0:T(8,128)}, u32[]{:S(2)}) copy-start(f32[128,256]{1,0:T(8,128)} %param.5) | copy-start | bytes 393220
  7.2 100.4 %all-gather.8.cloned.1.call-start = ((), (), s32[]{:S(2)}) async-start(), calls=%async_computation.1 | async-start | bytes 2228224 | tf_op jit(solution)/shard_map/all_gather | solution.py:71
  49.4 134.0 %all-gather.10.cloned.1.call-start = ((), (), s32[]{:S(2)}) async-start(), calls=%async_computation.2 | async-start | bytes 4325376 | tf_op jit(solution)/shard_map/all_gather | solution.py:73
  50.2 195.7 %all-gather.6.cloned.1.call-start = ((), (), s32[]{:S(2)}) async-start(), calls=%async_computation | async-start | bytes 2228224 | tf_op jit(solution)/shard_map/all_gather | solution.py:72
  50.9 270.1 %all-gather.12.cloned.1.call-start = ((), (), s32[]{:S(2)}) async-start(), calls=%async_computation.3 | async-start | bytes 4325376 | tf_op jit(solution)/shard_map/all_gather | solution.py:76
  189.1 196.6 %all-gather.14.cloned.1.call-start = ((), (), s32[]{:S(2)}) async-start(), calls=%async_computation.4 | async-start | bytes 2228224 | tf_op jit(solution)/shard_map/all_gather | solution.py:78
Sparse Core Ops, SparseCore 0:
  49.6 57.9 all-gather.7
  110.3 73.1 all-gather.9
  187.0 58.8 all-gather.5
  247.9 73.1 all-gather.11
  326.8 58.8 all-gather.13
where the time goes:
time: 398 us
  waiting for transfers between devices  324 us (81%)
  blocking collectives  37.2 us (9%)
  matrix products  16.7 us (4%)
  between operations  13.8 us (3%)
  other arithmetic  4.61 us (1%)
    all_gather x1, waiting for transfers between devices, body(): iterate_col = lax.all_gather(masked, 'row', axis=0, tiled=True)  75.9 us
    all_gather x1, waiting for transfers between devices, body(): lax.all_gather(product_one, 'row', axis=0, tiled=True)  75.1 us
    all_gather x1, waiting for transfers between devices, body(): second_row = lax.all_gather(product_two, 'col', axis=1, tiled=True)  59 us
    all_gather x1, waiting for transfers between devices, body(): iterate_row = lax.all_gather(masked, 'col', axis=1, tiled=True)  56.8 us
    all_gather x1, waiting for transfers between devices, body(): margin_row = lax.all_gather(margin, 'col', axis=1, tiled=True)  56.6 us
    all_gather x1, blocking collectives, body(): everyone = lax.all_gather(records, 'row', axis=1, tiled=True)  37.2 us
    dot_general x3, matrix products, matmul(): jnp.dot(left, right, precision=lax.Precision.HIGHEST, preferred_element_t...  16.7 us
  transfers between devices with their start and end apart: 5, of which 5 were waited for; matrix products, arithmetic and copies ran while one was open for 2% of the time, Pallas kernels for 0%

commit v1 on v0

--- a/solution.py
+++ b/solution.py
@@ -70,7 +70,9 @@
     masked = tile_mask * iterate
     margin_row = lax.all_gather(margin, "col", axis=1, tiled=True)
     iterate_row = lax.all_gather(masked, "col", axis=1, tiled=True)
-    iterate_col = lax.all_gather(masked, "row", axis=0, tiled=True)
+    iterate_col = jnp.concatenate(
+        lax.all_to_all(jnp.stack([masked] * lax.axis_size("row")), "row", 0, 0), axis=0
+    )
     product_one = tile_mask * matmul(margin_row, iterate_col)
     product_two = tile_mask * accumulate(
         iterate_row, lax.all_gather(product_one, "row", axis=0, tiled=True)

time: 398 us -> 516 us (1.30)
  blocking collectives: 37.2 us -> 207 us
  waiting for transfers between devices: 324 us -> 255 us
  starting transfers between devices: 0.2 us -> 15.9 us
    all_gather x1, blocking collectives: 37.2 us -> 207 us  [body(): everyone = lax.all_gather(records, 'row', axis=1, tiled=True)]
    all_gather x1 -> x0, waiting for transfers between devices: 75.9 us -> none  [body(): iterate_col = lax.all_gather(masked, 'row', axis=0, tiled=True)]
    all_to_all x0 -> x1, starting transfers between devices: none -> 15.7 us  [body(): lax.all_to_all(jnp.stack([masked] * lax.axis_size('row')), 'row', 0, 0)]
  transfers between devices with their start and end apart: 5 -> 5, of which waited for: 5 -> 4; matrix products, arithmetic and copies ran while one was open for 2% -> 2% of each run, Pallas kernels for 0% -> 0%
where the time goes in v1:
time: 516 us
  waiting for transfers between devices  255 us (49%)
  blocking collectives  207 us (40%)
  matrix products  16.7 us (3%)
  starting transfers between devices  15.9 us (3%)
  between operations  13.8 us (3%)
    all_gather x1, blocking collectives, body(): everyone = lax.all_gather(records, 'row', axis=1, tiled=True)  207 us
    all_gather x1, waiting for transfers between devices, body(): lax.all_gather(product_one, 'row', axis=0, tiled=True)  75.3 us
    all_gather x1, waiting for transfers between devices, body(): margin_row = lax.all_gather(margin, 'col', axis=1, tiled=True)  60.7 us
    all_gather x1, waiting for transfers between devices, body(): iterate_row = lax.all_gather(masked, 'col', axis=1, tiled=True)  59.7 us
    all_gather x1, waiting for transfers between devices, body(): second_row = lax.all_gather(product_two, 'col', axis=1, tiled=True)  59 us
    dot_general x3, matrix products, matmul(): jnp.dot(left, right, precision=lax.Precision.HIGHEST, preferred_element_t...  16.7 us
    all_to_all x1, starting transfers between devices, body(): lax.all_to_all(jnp.stack([masked] * lax.axis_size('row')), 'row', 0, 0)  15.7 us
  transfers between devices with their start and end apart: 5, of which 4 were waited for; matrix products, arithmetic and copies ran while one was open for 2% of the time, Pallas kernels for 0%

profile of v1, /device:TPU:2, one launch (start us, length us, event | category | flops | bytes accessed | tf_op | source)
XLA Modules:
  0.0 515.8 jit_solution(10527452703363746720)
XLA Ops:
  7.2 0.8 convert_bitcast_fusion
  7.9 0.1 broadcast_bitcast_fusion
  8.0 0.9 broadcast_multiply_fusion
  8.9 0.0 copy-start
  8.9 2.5 stack.2
  11.4 15.7 %all-to-all-start = ((f32[32,128,256]{2,1,0:T(8,128)}), f32[32,128,256]{2,1,0:T(8,128)}, u32[]{:S(2)}, u32[]{:S(2)}) async-start(f32[32,128,256]{2,1,0:T(8,128)} %stack.2), calls=%async_computation | async-start | bytes 8388608 | tf_op jit(solution)/shard_map/all_to_all | solution.py:74
  27.2 0.0 all-gather.7.cloned.1.call-start
  27.2 207.4 %all_gather.15 = f32[9,4096]{1,0:T(8,128)S(1)} all-gather(f32[9,128]{1,0:T(8,128)S(1)} %copy-done.2), channel_id=1, replica_groups=mesh['row'=32,'col'=16] {'row'}, dimensions={1}, use_global_device_ids=true | all-gather | bytes 152064 | tf_op jit(solution)/shard_map/all_gather | solution.py:59
  234.6 0.1 constant_dynamic-slice_fusion
  234.8 2.1 fusion.74
  237.0 0.0 all-gather.7.cloned.1.call-update
  237.0 0.0 all-gather.5.cloned.1.call-start
  237.0 0.7 all-gather.5.cloned.1.call-update
  237.7 0.0 all-gather.9.cloned.1.call-start
  237.8 60.7 %all-gather.7.cloned.1.call-done = f32[128,4096]{1,0:T(8,128)} async-done(((f32[128,256]{1,0:T(8,128)}), f32[128,4096]{1,0:T(8,128)}) %all-gather.7.cloned.1.call-update) | async-done | bytes 2097168 | tf_op jit(solution)/shard_map/all_gather | solution.py:71
  298.5 5.6 %convolution_multiply_fusion.2 = f32[128,256]{1,0:T(8,128)} fusion(f32[128,4096]{1,0:T(8,128)} %all-gather.7.cloned.1.call-done, f32[4096,256]{1,0:T(8,128)} %bitcast.21, f32[256]{0:T(256)S(1)} %broadcast_bitcast_fusion), kind=kOutput, calls=%fused_computation.4 | convolution fusion | flops 1610645504 | bytes 6423552 | tf_op jit(solution)/shard_map/dot_general | solution.py:46
  304.0 0.0 all-gather.9.cloned.1.call-update
  304.1 0.0 all-gather.11.cloned.1.call-start
  304.1 59.7 %all-gather.5.cloned.1.call-done = f32[128,4096]{1,0:T(8,128)} async-done(((f32[128,256]{1,0:T(8,128)}), f32[128,4096]{1,0:T(8,128)}) %all-gather.5.cloned.1.call-update) | async-done | bytes 2097168 | tf_op jit(solution)/shard_map/all_gather | solution.py:72
  363.9 75.3 %all-gather.9.cloned.1.call-done = f32[4096,256]{1,0:T(8,128)} async-done(((f32[128,256]{1,0:T(8,128)}), f32[4096,256]{1,0:T(8,128)}) %all-gather.9.cloned.1.call-update) | async-done | bytes 4194320 | tf_op jit(solution)/shard_map/all_gather | solution.py:78
  439.2 5.6 %convolution_multiply_fusion.1 = f32[128,256]{1,0:T(8,128)} fusion(f32[128,4096]{1,0:T(8,128)} %all-gather.5.cloned.1.call-done, f32[4096,256]{1,0:T(8,128)} %all-gather.9.cloned.1.call-done, f32[256]{0:T(256)S(1)} %broadcast_bitcast_fusion), kind=kOutput, calls=%fused_computation.3 | convolution fusion | flops 1610645504 | bytes 6423552 | tf_op jit(solution)/shard_map/dot_general | solution.py:46
  444.7 0.0 all-gather.11.cloned.1.call-update
  444.8 59.0 %all-gather.11.cloned.1.call-done = f32[128,4096]{1,0:T(8,128)} async-done(((f32[128,256]{1,0:T(8,128)}), f32[128,4096]{1,0:T(8,128)}) %all-gather.11.cloned.1.call-update) | async-done | bytes 2097168 | tf_op jit(solution)/shard_map/all_gather | solution.py:80
  503.7 5.6 %fusion.1 = f32[128,256]{1,0:T(8,128)} fusion(f32[128,4096]{1,0:T(8,128)} %all-gather.11.cloned.1.call-done, f32[4096,256]{1,0:T(8,128)} %bitcast.21, f32[256]{0:T(256)S(1)} %broadcast_bitcast_fusion, f32[128,256]{1,0:T(8,128)S(1)} %copy-done.1), kind=kOutput, calls=%fused_computation.2 | convolution fusion | flops 1610776576 | bytes 6554624 | tf_op jit(solution)/shard_map/dot_general | solution.py:46
  (8 shorter events, 0.1 us)
Async XLA Ops:
  8.9 2.5 copy-start
  11.4 15.8 %copy-start.2 = (f32[9,128]{1,0:T(8,128)S(1)}, f32[9,128]{1,0:T(8,128)}, u32[]{:S(2)}) copy-start(f32[9,128]{1,0:T(8,128)} %param.3) | copy-start | bytes 13828
  11.4 287.1 %all-to-all-start = ((f32[32,128,256]{2,1,0:T(8,128)}), f32[32,128,256]{2,1,0:T(8,128)}, u32[]{:S(2)}, u32[]{:S(2)}) async-start(f32[32,128,256]{2,1,0:T(8,128)} %stack.2), calls=%async_computation | async-start | bytes 8388608 | tf_op jit(solution)/shard_map/all_to_all | solution.py:74
  27.2 271.3 %all-gather.7.cloned.1.call-start = ((), (), s32[]{:S(2)}) async-start(), calls=%async_computation.2 | async-start | bytes 2228224 | tf_op jit(solution)/shard_map/all_gather | solution.py:71
  237.0 126.9 %all-gather.5.cloned.1.call-start = ((), (), s32[]{:S(2)}) async-start(), calls=%async_computation.1 | async-start | bytes 2228224 | tf_op jit(solution)/shard_map/all_gather | solution.py:72
  237.7 201.4 %all-gather.9.cloned.1.call-start = ((), (), s32[]{:S(2)}) async-start(), calls=%async_computation.3 | async-start | bytes 4325376 | tf_op jit(solution)/shard_map/all_gather | solution.py:78
  304.0 199.7 %copy-start.1 = (f32[128,256]{1,0:T(8,128)S(1)}, f32[128,256]{1,0:T(8,128)}, u32[]{:S(2)}) copy-start(f32[128,256]{1,0:T(8,128)} %param.5) | copy-start | bytes 393220
  304.1 199.7 %all-gather.11.cloned.1.call-start = ((), (), s32[]{:S(2)}) async-start(), calls=%async_computation.4 | async-start | bytes 2228224 | tf_op jit(solution)/shard_map/all_gather | solution.py:80
Sparse Core Ops, SparseCore 0:
  237.1 61.2 all-gather.6
  302.0 61.7 all-gather.4
  366.0 73.1 all-gather.8
  444.9 58.8 all-gather.10
